TPU v7x, 32 devices: a whole 2x2x4 slice. The times are simulated.
32 devices in a mesh: rep: 16 (over z, x, core), dom: 2 (over y).
Axes of the slice: x: 2, y: 2, z: 4, core: 2. Of those that a mesh axis runs over, the one named last changes fastest.
Arguments:
- field: float32 [16, 256, 2048], P('rep', 'dom'), may hold values from -2.5 to 2.5
- momentum: float32 [16, 256, 2048], P('rep', 'dom'), may hold values from -4 to 4
- labels: int32 [16], P('rep'), may hold values from 0 to 15, each once
- betas: float32 [16], replicated, may hold values from 0.4 to 1.6
- accept: int32 [16], P('rep'), may hold values 0 or 1
- swap_pairs: int32 [16], replicated, may hold values from 0 to 15, as said below
Outputs:
- field_out: float32 [16, 256, 2048], P('rep', 'dom')
- field_sorted: float32 [16, 256, 2048], P('rep', 'dom')
- labels_out: int32 [16], P('rep')
- energy_change: float32 [16], P('rep')
- ladder_action: float32 [16], P('rep')
Inputs may be any that keep to these rules, and one draw needn't show every extreme that they name: Each temperature index t is paired with itself, with t - 1 or with t + 1, and the pairing is symmetric: swap_pairs[swap_pairs[t]] = t. labels is a permutation of the temperature indices.
All inputs are finite; a program needn't handle non-finite values. No bound on the sum of `accept` on one device may be relied on, other than what follows from the above.
Results may differ from a plain program's by a relative error of at most 0.0003.
Values sent between devices are 32-bit elements; how exact they have to be, the bound alone decides.
No kernel may reach another device: no remote copies, remote signals or barrier semaphores. Data moves between devices by JAX's collectives and lax.ppermute only.
A program may use at most 64 MiB of HBM per device.

v0:
```python
import jax
import jax.numpy as jnp
from jax import lax
from jax.sharding import PartitionSpec as P

STEPS = 8
hopping = 0.18
quartic = 0.3
step_size = 0.05


def with_halo(cells, sides, width):
    for axis, dim in sides:
        count = lax.axis_size(axis)
        head = lax.slice_in_dim(cells, 0, width, axis=dim)
        tail = lax.slice_in_dim(cells, cells.shape[dim] - width, cells.shape[dim], axis=dim)
        cells = jnp.concatenate(
            [
                lax.ppermute(tail, axis, [(i, (i + 1) % count) for i in range(count)]),
                cells,
                lax.ppermute(head, axis, [((i + 1) % count, i) for i in range(count)]),
            ],
            axis=dim,
        )
    return cells


def force_rows(padded, coldness):
    centre = padded[1:-1]
    beside_all = padded[:-2] + padded[2:] + (jnp.roll(centre, 1, 1) + jnp.roll(centre, -1, 1))
    return coldness * (
        -2.0 * hopping * beside_all
        + 2.0 * centre
        + 4.0 * quartic * centre * (centre * centre - 1.0)
    )


def site_terms(padded, margin, strip_rows):
    values = padded[margin : margin + strip_rows]
    lower_row = padded[margin + 1 : margin + 1 + strip_rows]
    neighbours = lower_row + jnp.roll(values, -1, 1)
    squared = values * values
    return (
        -2.0 * hopping * values * neighbours + squared + quartic * (squared - 1.0) * (squared - 1.0)
    )


def trim_rows(values, margin, target):
    excess = margin - target
    return values[excess : values.shape[0] - excess]


def info_rows(label_value, action, members, lanes):
    pair = jnp.concatenate((label_value[None], action))
    front = jnp.broadcast_to(pair[None, None, :], (members, 1, 2))
    return jnp.concatenate((front, jnp.zeros((members, 1, lanes - 2), jnp.float32)), 2)


def body(field, momentum, labels, betas, accept, swap_pairs):
    strip_rows = field.shape[1]
    width = field.shape[2]
    ladder_index = jnp.arange(betas.shape[0], dtype=jnp.int32)
    chosen = ladder_index == labels[0]
    coldness = jnp.sum(jnp.where(chosen, betas, 0.0))
    new_label = jnp.sum(jnp.where(chosen, swap_pairs, 0))
    start_field = field[0]
    start_moment = momentum[0]
    current = start_field
    moment = start_moment
    margin = 0
    old_action = None
    new_action = None
    for leap_step in range(STEPS + 1):
        if margin == 0:
            stacked = with_halo(jnp.stack((current, moment)), (("dom", 1),), 3)
            current = stacked[0]
            moment = stacked[1]
            margin = 3
        padded = current
        outer = margin
        if leap_step == 0:
            old_action = site_terms(padded, outer, strip_rows)
        if leap_step == STEPS:
            new_action = site_terms(padded, outer, strip_rows)
        force_now = force_rows(padded, coldness)
        moment = trim_rows(moment, margin, outer - 1)
        current = trim_rows(padded, outer, outer - 1)
        margin = outer - 1
        factor = 0.5 * step_size if leap_step == 0 or leap_step == STEPS else step_size
        moment = moment - factor * force_now
        if leap_step < STEPS:
            current = current + step_size * moment
    change_part = jnp.sum(
        0.5 * moment * moment
        + coldness * new_action
        - (0.5 * start_moment * start_moment + coldness * old_action)
    )
    accepted = accept[0] == 1
    action_part = jnp.where(accepted, jnp.sum(new_action), jnp.sum(old_action))
    field_out = jnp.where(accepted, current, start_field)
    label_value = new_label.astype(jnp.float32)
    change, action = lax.psum((change_part[None], action_part[None]), "dom")
    members = lax.axis_size("rep")
    blocks = field_out.reshape(members, -1, width)
    outgoing = jnp.concatenate((blocks, info_rows(label_value, action, members, width)), 1)
    spread = lax.all_to_all(
        outgoing.reshape(1, -1, width), "rep", split_axis=1, concat_axis=0, tiled=True
    )
    label_values = spread[:, -1, 0]
    actions = spread[:, -1, 1]
    received = spread[:, :-1]
    held_labels = label_values.astype(jnp.int32)
    onehot = held_labels[None, :] == ladder_index[:, None]
    holder = jnp.sum(jnp.where(onehot, ladder_index[None, :], 0), 1)
    sites_total = lax.axis_size("dom") * strip_rows * width
    ladder_all = jnp.sum(jnp.where(onehot, actions[None, :], 0.0), 1) / sites_total
    ladder = lax.dynamic_slice_in_dim(ladder_all, lax.axis_index("rep"), 1)
    ordered = jnp.take(received, holder, axis=0)
    returned = lax.all_to_all(ordered, "rep", split_axis=0, concat_axis=1, tiled=True)
    return (field_out[None], returned, new_label[None], change, ladder)


def solution(mesh):
    placed = (P("rep", "dom", None), P("rep", "dom", None), P("rep"), P(), P("rep"), P())
    return jax.shard_map(
        body,
        mesh=mesh,
        in_specs=placed,
        out_specs=(P("rep", "dom", None), P("rep", "dom", None), P("rep"), P("rep"), P("rep")),
        check_vma=False,
    )
```

profile of v0, /device:TPU:9, one launch (start us, length us, event | category | flops | bytes accessed | tf_op | source)
XLA Modules:
  0.0 129.3 jit_solution(5219297042923690402)
XLA Ops:
  0.6 1.4 %constant_dynamic-update-slice_fusion.1 = f32[2,128,2048]{2,1,0:T(8,128)S(1)} fusion(f32[1,128,2048]{2,1,0:T(8,128)} %param.6), kind=kLoop, calls=%fused_computation.139 | loop fusion | bytes 2097152
  2.3 1.3 %collective-permute-start.1 = (f32[2,3,2048]{2,1,0:T(4,128)S(1)}, f32[2,3,2048]{2,1,0:T(4,128)S(1)}, u32[]{:S(2)}, u32[]{:S(2)}) collective-permute-start(f32[2,3,2048]{2,1,0:T(4,128)S(1)} %get-tuple-element.33), channel_id=1, source_target_pairs={{1,0},{0,1},{3,2},{2,3},{5,4},{4,5},{7,6},{6,7},{9,8},{8,9},{11,10... | collective-permute-start | bytes 147464 | tf_op jit(solution)/shard_map/ppermute | solution.py:21
  5.5 2.0 %collective-permute-done = f32[2,3,2048]{2,1,0:T(4,128)S(1)} collective-permute-done((f32[2,3,2048]{2,1,0:T(4,128)S(1)}, f32[2,3,2048]{2,1,0:T(4,128)S(1)}, u32[]{:S(2)}, u32[]{:S(2)}) %collective-permute-start) | collective-permute-done | bytes 49184 | tf_op jit(solution)/shard_map/ppermute | solution.py:19
  8.3 1.5 %multiply_add_fusion.5 = (f32[132,2048]{1,0:T(8,128)S(1)}, f32[132,2048]{1,0:T(8,128)S(1)}) fusion(f32[2,134,2048]{2,1,0:T(8,128)S(1)} %pad_maximum_fusion, f32[132,1]{1,0:T(8,128)S(1)} %get-tuple-element.70, f32[132,2047]{1,0:T(8,128)S(1)} %get-tuple-element.72, f32[132,2047]{1,0:T(8,128)S(1)} %get-tuple-element.71, f32[132,1]{1,0:T(8,128)S(1)} %get-tuple-element.69, ...), kind=kLoop, calls=%fused_computation.77 | loop fusion | flops 4866048 | bytes 8650756 | tf_op jit(solution)/shard_map/add | solution.py:92
  10.4 1.5 %multiply_add_fusion.4 = (f32[130,2048]{1,0:T(8,128)S(1)}, f32[130,2048]{1,0:T(8,128)S(1)}) fusion(f32[132,2048]{1,0:T(8,128)S(1)} %get-tuple-element.24, f32[130,1]{1,0:T(8,128)S(1)} %get-tuple-element.66, f32[130,2047]{1,0:T(8,128)S(1)} %get-tuple-element.68, f32[130,2047]{1,0:T(8,128)S(1)} %get-tuple-element.67, f32[130,1]{1,0:T(8,128)S(1)} %get-tuple-element.65, ...), kind=kLoop, calls=%fused_computation.76 | loop fusion | flops 4792320 | bytes 8519684 | tf_op jit(solution)/shard_map/add | solution.py:92
  12.4 1.5 %add_bitcast_fusion.1 = (f32[1,128,2048]{2,1,0:T(8,128)S(1)}, f32[128,2048]{1,0:T(8,128)S(1)}) fusion(f32[130,2048]{1,0:T(8,128)S(1)} %get-tuple-element.22, f32[128,1]{1,0:T(8,128)S(1)} %get-tuple-element.62, f32[128,2047]{1,0:T(8,128)S(1)} %get-tuple-element.64, f32[128,2047]{1,0:T(8,128)S(1)} %get-tuple-element.63, f32[128,1]{1,0:T(8,128)S(1)} %get-tuple-element.61, ...), kind=kLoop, calls=%fused_computation.120 | loop fusion | flops 4718592 | bytes 8388612 | tf_op jit(solution)/shard_map/stack | solution.py:75
  14.4 1.0 collective-permute-start.3
  15.4 1.6 %collective-permute-done.2 = f32[2,3,2048]{2,1,0:T(4,128)S(1)} collective-permute-done((f32[2,3,2048]{2,1,0:T(4,128)S(1)}, f32[2,3,2048]{2,1,0:T(4,128)S(1)}, u32[]{:S(2)}, u32[]{:S(2)}) %collective-permute-start.2) | collective-permute-done | bytes 49184 | tf_op jit(solution)/shard_map/ppermute | solution.py:19
  17.1 0.7 collective-permute-done.3
  18.7 1.5 %multiply_add_fusion.3 = (f32[132,2048]{1,0:T(8,128)S(1)}, f32[132,2048]{1,0:T(8,128)S(1)}) fusion(f32[2,134,2048]{2,1,0:T(8,128)S(1)} %pad_maximum_fusion.1, f32[132,1]{1,0:T(8,128)S(1)} %get-tuple-element.58, f32[132,2047]{1,0:T(8,128)S(1)} %get-tuple-element.60, f32[132,2047]{1,0:T(8,128)S(1)} %get-tuple-element.59, f32[132,1]{1,0:T(8,128)S(1)} %get-tuple-element.57, ...), kind=kLoop, calls=%fused_computation.75 | loop fusion | flops 4866048 | bytes 8650756 | tf_op jit(solution)/shard_map/add | solution.py:92
  20.7 1.5 %multiply_add_fusion.2 = (f32[130,2048]{1,0:T(8,128)S(1)}, f32[130,2048]{1,0:T(8,128)S(1)}) fusion(f32[132,2048]{1,0:T(8,128)S(1)} %get-tuple-element.18, f32[130,1]{1,0:T(8,128)S(1)} %get-tuple-element.54, f32[130,2047]{1,0:T(8,128)S(1)} %get-tuple-element.56, f32[130,2047]{1,0:T(8,128)S(1)} %get-tuple-element.55, f32[130,1]{1,0:T(8,128)S(1)} %get-tuple-element.53, ...), kind=kLoop, calls=%fused_computation.74 | loop fusion | flops 4792320 | bytes 8519684 | tf_op jit(solution)/shard_map/add | solution.py:92
  22.8 1.5 %add_bitcast_fusion = (f32[1,128,2048]{2,1,0:T(8,128)S(1)}, f32[128,2048]{1,0:T(8,128)S(1)}) fusion(f32[130,2048]{1,0:T(8,128)S(1)} %get-tuple-element.16, f32[128,1]{1,0:T(8,128)S(1)} %get-tuple-element.50, f32[128,2047]{1,0:T(8,128)S(1)} %get-tuple-element.52, f32[128,2047]{1,0:T(8,128)S(1)} %get-tuple-element.51, f32[128,1]{1,0:T(8,128)S(1)} %get-tuple-element.49, ...), kind=kLoop, calls=%fused_computation.119 | loop fusion | flops 4718592 | bytes 8388612 | tf_op jit(solution)/shard_map/stack | solution.py:75
  24.3 0.9 copy-done.1
  25.6 0.8 collective-permute-start.4
  27.7 1.3 %slice.515 = f32[128,2047]{1,0:T(8,128)} slice(f32[128,2048]{1,0:T(8,128)S(1)} %bitcast.130), slice={[0:128], [1:2048]} | slice | bytes 2096128 | tf_op jit(solution)/shard_map/jit(_roll_static)/slice | solution.py:41
  30.3 1.9 %pad_maximum_fusion.2 = f32[2,134,2048]{2,1,0:T(8,128)S(1)} fusion(f32[2,3,2048]{2,1,0:T(4,128)S(1)} %collective-permute-done.5, f32[1,128,2048]{2,1,0:T(8,128)} %bitcast.133, f32[1,128,2048]{2,1,0:T(8,128)} %copy-done.1, f32[2,3,2048]{2,1,0:T(4,128)S(1)} %collective-permute-done.4), kind=kLoop, calls=%fused_computation.3 | loop fusion | flops 1646592 | bytes 4390912 | tf_op jit(solution)/shard_map/concatenate | solution.py:17
  32.8 1.5 %multiply_add_fusion.1 = (f32[132,2048]{1,0:T(8,128)S(1)}, f32[132,2048]{1,0:T(8,128)S(1)}) fusion(f32[2,134,2048]{2,1,0:T(8,128)S(1)} %pad_maximum_fusion.2, f32[132,1]{1,0:T(8,128)S(1)} %get-tuple-element.46, f32[132,2047]{1,0:T(8,128)S(1)} %get-tuple-element.48, f32[132,2047]{1,0:T(8,128)S(1)} %get-tuple-element.47, f32[132,1]{1,0:T(8,128)S(1)} %get-tuple-element.45, ...), kind=kLoop, calls=%fused_computation.73 | loop fusion | flops 4866048 | bytes 8650756 | tf_op jit(solution)/shard_map/add | solution.py:92
  34.8 1.7 %multiply_add_fusion = (f32[130,2048]{1,0:T(8,128)S(1)}, f32[130,2048]{1,0:T(8,128)S(1)}) fusion(f32[132,2048]{1,0:T(8,128)S(1)} %get-tuple-element.12, f32[130,1]{1,0:T(8,128)S(1)} %get-tuple-element.42, f32[130,2047]{1,0:T(8,128)S(1)} %get-tuple-element.44, f32[130,2047]{1,0:T(8,128)S(1)} %get-tuple-element.43, f32[130,1]{1,0:T(8,128)S(1)} %get-tuple-element.41, ...), kind=kLoop, calls=%fused_computation.72 | loop fusion | flops 4792320 | bytes 8519684 | tf_op jit(solution)/shard_map/add | solution.py:92
  37.0 0.7 copy-done.4
  38.1 4.7 %fusion.77 = (f32[16,8,2048]{2,1,0:T(8,128)}, f32[1,128,2048]{2,1,0:T(8,128)}, f32[]{:T(128)}, f32[]{:T(128)}, f32[]{:T(128)}) fusion(f32[130,2048]{1,0:T(8,128)S(1)} %get-tuple-element.10, pred[]{:T(512)} %bitcast, f32[1,128,2048]{2,1,0:T(8,128)S(1)} %copy-done, f32[1,128,2048]{2,1,0:T(8,128)S(1)} %copy-done.4, f32[128,1]{1,0:T(8,128)S(1)} %get-tuple-element.39, ...), kind=kLoop, calls=%fused_computation.123 | loop fusion | flops 12320765 | bytes 13680657 | tf_op jit(solution)/shard_map/reshape | solution.py:104
  44.0 4.9 %all-reduce.1 = (f32[1]{0:T(128)}, f32[1]{0:T(128)}) all-reduce(f32[1]{0:T(128)} %bitcast.20, f32[1]{0:T(128)} %bitcast.26), channel_id=1, replica_groups=mesh['rep'=16,'dom'=2] {'dom'}, use_global_device_ids=true, to_apply=%region_4.5 | all-reduce | flops 2 | bytes 16 | tf_op jit(solution)/shard_map/psum | solution.py:102
  48.9 0.7 select_maximum_fusion
  49.7 1.5 %pad_maximum_fusion.3 = f32[16,9,2048]{2,1,0:T(8,128)S(1)} fusion(f32[16,1,2048]{2,1,0:T(1,128)S(1)} %concatenate.111, f32[16,8,2048]{2,1,0:T(8,128)} %get-tuple-element.26), kind=kLoop, calls=%fused_computation.4 | loop fusion | flops 294912 | bytes 2359296 | tf_op jit(solution)/shard_map/concatenate | solution.py:105
  51.2 1.4 %reshape.79 = f32[1,144,2048]{2,0,1:T(1,128)S(1)} reshape(f32[16,9,2048]{2,1,0:T(8,128)S(1)} %pad_maximum_fusion.3) | data formatting | bytes 2359296 | tf_op jit(solution)/shard_map/reshape | solution.py:107
  52.6 38.6 %all_to_all.24 = f32[1,144,2048]{2,0,1:T(1,128)S(1)} all-to-all(f32[1,144,2048]{2,0,1:T(1,128)S(1)} %reshape.79), channel_id=1, replica_groups=mesh['rep'=16,'dom'=2] {'rep'}, dimensions={1} | all-to-all | bytes 2359296 | tf_op jit(solution)/shard_map/all_to_all | solution.py:106
  91.2 2.8 %reduce = f32[144,2048]{1,0:T(8,128)S(1)} reduce(f32[1,144,2048]{2,0,1:T(1,128)S(1)} %all_to_all.24, f32[]{:T(128)} %constant.76), dimensions={0}, to_apply=%all_to_all.8.reduce_sub_computation | reduce | bytes 2359300 | tf_op jit(solution)/shard_map/all_to_all | solution.py:106
  94.5 1.0 slice.518
  95.7 1.8 %gather_fusion = f32[16,8,2048]{2,1,0:T(8,128)S(1)} fusion(f32[16,8,2048]{2,1,0:T(8,128)} %slice.518, s32[1024]{0:T(1024)S(1)} %pad_clamp_fusion), kind=kCustom, calls=%fused_computation | custom fusion | bytes 2097216 | tf_op jit(solution)/shard_map/jit(_take)/gather | solution.py:118
  97.6 1.1 broadcast_select_fusion
  98.7 4.7 %all-to-all-start.1 = ((f32[16,8,2048]{2,1,0:T(8,128)}), f32[16,8,2048]{2,1,0:T(8,128)S(1)}, u32[]{:S(2)}, u32[]{:S(2)}) async-start(f32[16,8,2048]{2,1,0:T(8,128)} %broadcast_select_fusion), calls=%async_computation.1 | async-start | bytes 2097152 | tf_op jit(solution)/shard_map/all_to_all | solution.py:119
  104.4 23.9 %all-to-all-done.1 = f32[16,8,2048]{2,1,0:T(8,128)S(1)} async-done(((f32[16,8,2048]{2,1,0:T(8,128)}), f32[16,8,2048]{2,1,0:T(8,128)S(1)}, u32[]{:S(2)}, u32[]{:S(2)}) %all-to-all-start.1) | async-done | bytes 1048608 | tf_op jit(solution)/shard_map/all_to_all | solution.py:119
  128.3 1.0 copy.19
  (61 shorter events, 11.0 us)
Async XLA Ops:
  0.6 1.5 %copy-start.3 = (f32[1,128,2048]{2,1,0:T(8,128)S(1)}, f32[1,128,2048]{2,1,0:T(8,128)}, u32[]{:S(2)}) copy-start(f32[1,128,2048]{2,1,0:T(8,128)} %param.7) | copy-start | bytes 3145732
  2.2 2.3 %copy-start.6 = (f32[16]{0:T(128)S(1)}, f32[16]{0:T(128)}, u32[]{:S(2)}) copy-start(f32[16]{0:T(128)} %param.9) | copy-start | bytes 196
  2.3 3.2 %collective-permute-start.1 = (f32[2,3,2048]{2,1,0:T(4,128)S(1)}, f32[2,3,2048]{2,1,0:T(4,128)S(1)}, u32[]{:S(2)}, u32[]{:S(2)}) collective-permute-start(f32[2,3,2048]{2,1,0:T(4,128)S(1)} %get-tuple-element.33), channel_id=1, source_target_pairs={{1,0},{0,1},{3,2},{2,3},{5,4},{4,5},{7,6},{6,7},{9,8},{8,9},{11,10... | collective-permute-start | bytes 147464 | tf_op jit(solution)/shard_map/ppermute | solution.py:21
  3.6 3.9 %collective-permute-start = (f32[2,3,2048]{2,1,0:T(4,128)S(1)}, f32[2,3,2048]{2,1,0:T(4,128)S(1)}, u32[]{:S(2)}, u32[]{:S(2)}) collective-permute-start(f32[2,3,2048]{2,1,0:T(4,128)S(1)} %get-tuple-element.32), channel_id=1, source_target_pairs={{0,1},{1,0},{2,3},{3,2},{4,5},{5,4},{6,7},{7,6},{8,9},{9,8},{10,11... | collective-permute-start | bytes 147464 | tf_op jit(solution)/shard_map/ppermute | solution.py:19
  13.9 3.2 %collective-permute-start.2 = (f32[2,3,2048]{2,1,0:T(4,128)S(1)}, f32[2,3,2048]{2,1,0:T(4,128)S(1)}, u32[]{:S(2)}, u32[]{:S(2)}) collective-permute-start(f32[2,3,2048]{2,1,0:T(4,128)S(1)} %get-tuple-element.30), channel_id=1, source_target_pairs={{0,1},{1,0},{2,3},{3,2},{4,5},{5,4},{6,7},{7,6},{8,9},{9,8},{10,11... | collective-permute-start | bytes 147464 | tf_op jit(solution)/shard_map/ppermute | solution.py:19
  14.4 3.3 %collective-permute-start.3 = (f32[2,3,2048]{2,1,0:T(4,128)S(1)}, f32[2,3,2048]{2,1,0:T(4,128)S(1)}, u32[]{:S(2)}, u32[]{:S(2)}) collective-permute-start(f32[2,3,2048]{2,1,0:T(4,128)S(1)} %get-tuple-element.31), channel_id=1, source_target_pairs={{1,0},{0,1},{3,2},{2,3},{5,4},{4,5},{7,6},{6,7},{9,8},{8,9},{11,10... | collective-permute-start | bytes 147464 | tf_op jit(solution)/shard_map/ppermute | solution.py:21
  24.2 1.0 copy-start.1
  24.2 1.3 %copy-start.2 = (f32[128,2048]{1,0:T(8,128)}, f32[128,2048]{1,0:T(8,128)S(1)}, u32[]{:S(2)}) copy-start(f32[128,2048]{1,0:T(8,128)S(1)} %get-tuple-element.15) | copy-start | bytes 3145732
  24.3 2.8 %copy-start.7 = (s32[16]{0:T(128)S(1)}, s32[16]{0:T(128)}, u32[]{:S(2)}) copy-start(s32[16]{0:T(128)} %param.11) | copy-start | bytes 196
  24.3 3.4 %copy-start = (f32[1,128,2048]{2,1,0:T(8,128)S(1)}, f32[1,128,2048]{2,1,0:T(8,128)}, u32[]{:S(2)}) copy-start(f32[1,128,2048]{2,1,0:T(8,128)} %param.6) | copy-start | bytes 3145732
  25.6 4.7 %collective-permute-start.4 = (f32[2,3,2048]{2,1,0:T(4,128)S(1)}, f32[2,3,2048]{2,1,0:T(4,128)S(1)}, u32[]{:S(2)}, u32[]{:S(2)}) collective-permute-start(f32[2,3,2048]{2,1,0:T(4,128)S(1)} %get-tuple-element.28), channel_id=1, source_target_pairs={{0,1},{1,0},{2,3},{3,2},{4,5},{5,4},{6,7},{7,6},{8,9},{9,8},{10,11... | collective-permute-start | bytes 147464 | tf_op jit(solution)/shard_map/ppermute | solution.py:19
  26.3 4.0 %collective-permute-start.5 = (f32[2,3,2048]{2,1,0:T(4,128)S(1)}, f32[2,3,2048]{2,1,0:T(4,128)S(1)}, u32[]{:S(2)}, u32[]{:S(2)}) collective-permute-start(f32[2,3,2048]{2,1,0:T(4,128)S(1)} %get-tuple-element.29), channel_id=1, source_target_pairs={{1,0},{0,1},{3,2},{2,3},{5,4},{4,5},{7,6},{6,7},{9,8},{8,9},{11,10... | collective-permute-start | bytes 147464 | tf_op jit(solution)/shard_map/ppermute | solution.py:21
  36.5 1.2 copy-start.4
  36.5 1.5 %copy-start.5 = (f32[128,2047]{1,0:T(8,128)S(1)}, f32[128,2047]{1,0:T(8,128)}, u32[]{:S(2)}) copy-start(f32[128,2047]{1,0:T(8,128)} %slice.515) | copy-start | bytes 3144196
  98.7 29.6 %all-to-all-start.1 = ((f32[16,8,2048]{2,1,0:T(8,128)}), f32[16,8,2048]{2,1,0:T(8,128)S(1)}, u32[]{:S(2)}, u32[]{:S(2)}) async-start(f32[16,8,2048]{2,1,0:T(8,128)} %broadcast_select_fusion), calls=%async_computation.1 | async-start | bytes 2097152 | tf_op jit(solution)/shard_map/all_to_all | solution.py:119
where the time goes:
time: 130 us; the launch traced here: 129 us
  blocking collectives  43.5 us (33%)
  waiting for transfers between devices  28.7 us (22%)
  other arithmetic  27.5 us (21%)
  local copies, waits for them, and re-layouts  16.2 us (12%)
  starting transfers between devices  9.18 us (7%)
  between operations  4.24 us (3%)
    all_to_all x1, blocking collectives, body(): lax.all_to_all(outgoing.reshape(1, -1, width), 'rep', split_axis=1, conca...  38.6 us
    all_to_all x1, waiting for transfers between devices, body(): lax.all_to_all(ordered, 'rep', split_axis=0, concat_axis=1, tiled=True)  23.9 us
    add x6, other arithmetic, body(): current = current + step_size * moment  9.39 us
    psum x1, blocking collectives, body(): change, action = lax.psum((change_part[None], action_part[None]), 'dom')  4.91 us
    unnamed x18, local copies, waits for them, and re-layouts  4.81 us
    reshape x1, other arithmetic, body(): blocks = field_out.reshape(members, -1, width)  4.67 us
    all_to_all x1, starting transfers between devices, body(): lax.all_to_all(ordered, 'rep', split_axis=0, concat_axis=1, tiled=True)  4.66 us
    slice x16, local copies, waits for them, and re-layouts, force_rows(): jnp.roll(centre, 1, 1) + jnp.roll(centre, -1, 1)  3.78 us
  transfers between devices with their start and end apart: 7, of which 5 were waited for; matrix products, arithmetic and copies ran while one was open for 3% of the time, Pallas kernels for 0%

commit v1 on v0

--- a/solution.py
+++ b/solution.py
@@ -116,7 +116,10 @@
     ladder_all = jnp.sum(jnp.where(onehot, actions[None, :], 0.0), 1) / sites_total
     ladder = lax.dynamic_slice_in_dim(ladder_all, lax.axis_index("rep"), 1)
     ordered = jnp.take(received, holder, axis=0)
-    returned = lax.all_to_all(ordered, "rep", split_axis=0, concat_axis=1, tiled=True)
+    returned = jnp.concatenate(
+        lax.all_to_all(jnp.stack(jnp.split(ordered, lax.axis_size("rep"), axis=0)), "rep", 0, 0),
+        axis=1,
+    )
     return (field_out[None], returned, new_label[None], change, ladder)
 
 

time: 130 us -> 139 us (1.069)
  local copies, waits for them, and re-layouts: 16.2 us -> 26.4 us
    unnamed x18 -> x33, local copies, waits for them, and re-layouts: 4.81 us -> 14.3 us
where the time goes in v1:
time: 139 us
  blocking collectives  43.5 us (31%)
  waiting for transfers between devices  28.7 us (21%)
  other arithmetic  26.6 us (19%)
  local copies, waits for them, and re-layouts  26.4 us (19%)
  starting transfers between devices  9.18 us (7%)
  between operations  4.26 us (3%)
    all_to_all x1, blocking collectives, body(): lax.all_to_all(outgoing.reshape(1, -1, width), 'rep', split_axis=1, conca...  38.6 us
    all_to_all x1, waiting for transfers between devices, body(): lax.all_to_all(jnp.stack(jnp.split(ordered, lax.axis_size('rep'), axis=0)...  23.9 us
    unnamed x33, local copies, waits for them, and re-layouts  14.3 us
    add x6, other arithmetic, body(): current = current + step_size * moment  9.39 us
    psum x1, blocking collectives, body(): change, action = lax.psum((change_part[None], action_part[None]), 'dom')  4.91 us
    reshape x1, other arithmetic, body(): blocks = field_out.reshape(members, -1, width)  4.67 us
    all_to_all x1, starting transfers between devices, body(): lax.all_to_all(jnp.stack(jnp.split(ordered, lax.axis_size('rep'), axis=0)...  4.66 us
    slice x16, local copies, waits for them, and re-layouts, force_rows(): jnp.roll(centre, 1, 1) + jnp.roll(centre, -1, 1)  3.78 us
  transfers between devices with their start and end apart: 7, of which 5 were waited for; matrix products, arithmetic and copies ran while one was open for 3% of the time, Pallas kernels for 0%

profile of v1, /device:TPU:9, one launch (start us, length us, event | category | flops | bytes accessed | tf_op | source)
XLA Modules:
  0.0 138.6 jit_solution(5427600131527151947)
XLA Ops:
  0.6 1.4 %constant_dynamic-update-slice_fusion.1 = f32[2,128,2048]{2,1,0:T(8,128)S(1)} fusion(f32[1,128,2048]{2,1,0:T(8,128)} %param.6), kind=kLoop, calls=%fused_computation.162 | loop fusion | bytes 2097152
  2.3 1.3 collective-permute-start.1
  5.5 2.0 %collective-permute-done = f32[2,3,2048]{2,1,0:T(4,128)S(1)} collective-permute-done((f32[2,3,2048]{2,1,0:T(4,128)S(1)}, f32[2,3,2048]{2,1,0:T(4,128)S(1)}, u32[]{:S(2)}, u32[]{:S(2)}) %collective-permute-start) | collective-permute-done | bytes 49184 | tf_op jit(solution)/shard_map/ppermute | solution.py:19
  8.4 1.5 %multiply_add_fusion.5 = (f32[132,2048]{1,0:T(8,128)S(1)}, f32[132,2048]{1,0:T(8,128)S(1)}) fusion(f32[2,134,2048]{2,1,0:T(8,128)S(1)} %pad_maximum_fusion, f32[132,1]{1,0:T(8,128)S(1)} %get-tuple-element.70, f32[132,2047]{1,0:T(8,128)S(1)} %get-tuple-element.72, f32[132,2047]{1,0:T(8,128)S(1)} %get-tuple-element.71, f32[132,1]{1,0:T(8,128)S(1)} %get-tuple-element.69, ...), kind=kLoop, calls=%fused_computation.77 | loop fusion | flops 4866048 | bytes 8650756 | tf_op jit(solution)/shard_map/add | solution.py:92
  10.5 1.5 %multiply_add_fusion.4 = (f32[130,2048]{1,0:T(8,128)S(1)}, f32[130,2048]{1,0:T(8,128)S(1)}) fusion(f32[132,2048]{1,0:T(8,128)S(1)} %get-tuple-element.24, f32[130,1]{1,0:T(8,128)S(1)} %get-tuple-element.66, f32[130,2047]{1,0:T(8,128)S(1)} %get-tuple-element.68, f32[130,2047]{1,0:T(8,128)S(1)} %get-tuple-element.67, f32[130,1]{1,0:T(8,128)S(1)} %get-tuple-element.65, ...), kind=kLoop, calls=%fused_computation.76 | loop fusion | flops 4792320 | bytes 8519684 | tf_op jit(solution)/shard_map/add | solution.py:92
  12.5 1.5 %add_bitcast_fusion.1 = (f32[1,128,2048]{2,1,0:T(8,128)S(1)}, f32[128,2048]{1,0:T(8,128)S(1)}) fusion(f32[130,2048]{1,0:T(8,128)S(1)} %get-tuple-element.22, f32[128,1]{1,0:T(8,128)S(1)} %get-tuple-element.62, f32[128,2047]{1,0:T(8,128)S(1)} %get-tuple-element.64, f32[128,2047]{1,0:T(8,128)S(1)} %get-tuple-element.63, f32[128,1]{1,0:T(8,128)S(1)} %get-tuple-element.61, ...), kind=kLoop, calls=%fused_computation.120 | loop fusion | flops 4718592 | bytes 8388612 | tf_op jit(solution)/shard_map/stack | solution.py:75
  14.6 1.0 collective-permute-start.3
  15.5 1.6 %collective-permute-done.2 = f32[2,3,2048]{2,1,0:T(4,128)S(1)} collective-permute-done((f32[2,3,2048]{2,1,0:T(4,128)S(1)}, f32[2,3,2048]{2,1,0:T(4,128)S(1)}, u32[]{:S(2)}, u32[]{:S(2)}) %collective-permute-start.2) | collective-permute-done | bytes 49184 | tf_op jit(solution)/shard_map/ppermute | solution.py:19
  17.2 0.7 collective-permute-done.3
  18.8 1.5 %multiply_add_fusion.3 = (f32[132,2048]{1,0:T(8,128)S(1)}, f32[132,2048]{1,0:T(8,128)S(1)}) fusion(f32[2,134,2048]{2,1,0:T(8,128)S(1)} %pad_maximum_fusion.1, f32[132,1]{1,0:T(8,128)S(1)} %get-tuple-element.58, f32[132,2047]{1,0:T(8,128)S(1)} %get-tuple-element.60, f32[132,2047]{1,0:T(8,128)S(1)} %get-tuple-element.59, f32[132,1]{1,0:T(8,128)S(1)} %get-tuple-element.57, ...), kind=kLoop, calls=%fused_computation.75 | loop fusion | flops 4866048 | bytes 8650756 | tf_op jit(solution)/shard_map/add | solution.py:92
  20.9 1.5 %multiply_add_fusion.2 = (f32[130,2048]{1,0:T(8,128)S(1)}, f32[130,2048]{1,0:T(8,128)S(1)}) fusion(f32[132,2048]{1,0:T(8,128)S(1)} %get-tuple-element.18, f32[130,1]{1,0:T(8,128)S(1)} %get-tuple-element.54, f32[130,2047]{1,0:T(8,128)S(1)} %get-tuple-element.56, f32[130,2047]{1,0:T(8,128)S(1)} %get-tuple-element.55, f32[130,1]{1,0:T(8,128)S(1)} %get-tuple-element.53, ...), kind=kLoop, calls=%fused_computation.74 | loop fusion | flops 4792320 | bytes 8519684 | tf_op jit(solution)/shard_map/add | solution.py:92
  22.9 1.5 %add_bitcast_fusion = (f32[1,128,2048]{2,1,0:T(8,128)S(1)}, f32[128,2048]{1,0:T(8,128)S(1)}) fusion(f32[130,2048]{1,0:T(8,128)S(1)} %get-tuple-element.16, f32[128,1]{1,0:T(8,128)S(1)} %get-tuple-element.50, f32[128,2047]{1,0:T(8,128)S(1)} %get-tuple-element.52, f32[128,2047]{1,0:T(8,128)S(1)} %get-tuple-element.51, f32[128,1]{1,0:T(8,128)S(1)} %get-tuple-element.49, ...), kind=kLoop, calls=%fused_computation.119 | loop fusion | flops 4718592 | bytes 8388612 | tf_op jit(solution)/shard_map/stack | solution.py:75
  24.4 0.9 copy-done.1
  25.7 0.8 collective-permute-start.4
  26.4 0.7 collective-permute-start.5
  27.8 1.3 slice.515
  30.4 1.9 %pad_maximum_fusion.2 = f32[2,134,2048]{2,1,0:T(8,128)S(1)} fusion(f32[2,3,2048]{2,1,0:T(4,128)S(1)} %collective-permute-done.5, f32[1,128,2048]{2,1,0:T(8,128)} %bitcast.197, f32[1,128,2048]{2,1,0:T(8,128)} %copy-done.1, f32[2,3,2048]{2,1,0:T(4,128)S(1)} %collective-permute-done.4), kind=kLoop, calls=%fused_computation.3 | loop fusion | flops 1646592 | bytes 4390912 | tf_op jit(solution)/shard_map/concatenate | solution.py:17
  32.9 1.5 %multiply_add_fusion.1 = (f32[132,2048]{1,0:T(8,128)S(1)}, f32[132,2048]{1,0:T(8,128)S(1)}) fusion(f32[2,134,2048]{2,1,0:T(8,128)S(1)} %pad_maximum_fusion.2, f32[132,1]{1,0:T(8,128)S(1)} %get-tuple-element.46, f32[132,2047]{1,0:T(8,128)S(1)} %get-tuple-element.48, f32[132,2047]{1,0:T(8,128)S(1)} %get-tuple-element.47, f32[132,1]{1,0:T(8,128)S(1)} %get-tuple-element.45, ...), kind=kLoop, calls=%fused_computation.73 | loop fusion | flops 4866048 | bytes 8650756 | tf_op jit(solution)/shard_map/add | solution.py:92
  34.9 1.7 %multiply_add_fusion = (f32[130,2048]{1,0:T(8,128)S(1)}, f32[130,2048]{1,0:T(8,128)S(1)}) fusion(f32[132,2048]{1,0:T(8,128)S(1)} %get-tuple-element.12, f32[130,1]{1,0:T(8,128)S(1)} %get-tuple-element.42, f32[130,2047]{1,0:T(8,128)S(1)} %get-tuple-element.44, f32[130,2047]{1,0:T(8,128)S(1)} %get-tuple-element.43, f32[130,1]{1,0:T(8,128)S(1)} %get-tuple-element.41, ...), kind=kLoop, calls=%fused_computation.72 | loop fusion | flops 4792320 | bytes 8519684 | tf_op jit(solution)/shard_map/add | solution.py:92
  37.2 0.7 copy-done.4
  38.2 4.7 %fusion.77 = (f32[16,8,2048]{2,1,0:T(8,128)}, f32[1,128,2048]{2,1,0:T(8,128)}, f32[]{:T(128)}, f32[]{:T(128)}, f32[]{:T(128)}) fusion(f32[130,2048]{1,0:T(8,128)S(1)} %get-tuple-element.10, pred[]{:T(512)} %bitcast, f32[1,128,2048]{2,1,0:T(8,128)S(1)} %copy-done, f32[1,128,2048]{2,1,0:T(8,128)S(1)} %copy-done.4, f32[128,1]{1,0:T(8,128)S(1)} %get-tuple-element.39, ...), kind=kLoop, calls=%fused_computation.123 | loop fusion | flops 12320765 | bytes 13680657 | tf_op jit(solution)/shard_map/reshape | solution.py:104
  44.1 4.9 %all-reduce.1 = (f32[1]{0:T(128)}, f32[1]{0:T(128)}) all-reduce(f32[1]{0:T(128)} %bitcast.20, f32[1]{0:T(128)} %bitcast.42), channel_id=1, replica_groups=mesh['rep'=16,'dom'=2] {'dom'}, use_global_device_ids=true, to_apply=%region_4.5 | all-reduce | flops 2 | bytes 16 | tf_op jit(solution)/shard_map/psum | solution.py:102
  49.0 0.7 select_maximum_fusion
  49.8 1.5 %pad_maximum_fusion.3 = f32[16,9,2048]{2,1,0:T(8,128)S(1)} fusion(f32[16,1,2048]{2,1,0:T(1,128)S(1)} %concatenate.111, f32[16,8,2048]{2,1,0:T(8,128)} %get-tuple-element.26), kind=kLoop, calls=%fused_computation.4 | loop fusion | flops 294912 | bytes 2359296 | tf_op jit(solution)/shard_map/concatenate | solution.py:105
  51.3 1.4 %reshape.80 = f32[1,144,2048]{2,0,1:T(1,128)S(1)} reshape(f32[16,9,2048]{2,1,0:T(8,128)S(1)} %pad_maximum_fusion.3) | data formatting | bytes 2359296 | tf_op jit(solution)/shard_map/reshape | solution.py:107
  52.8 38.6 %all_to_all.17 = f32[1,144,2048]{2,0,1:T(1,128)S(1)} all-to-all(f32[1,144,2048]{2,0,1:T(1,128)S(1)} %reshape.80), channel_id=1, replica_groups=mesh['rep'=16,'dom'=2] {'rep'}, dimensions={1} | all-to-all | bytes 2359296 | tf_op jit(solution)/shard_map/all_to_all | solution.py:106
  91.3 2.8 %reduce = f32[144,2048]{1,0:T(8,128)S(1)} reduce(f32[1,144,2048]{2,0,1:T(1,128)S(1)} %all_to_all.17, f32[]{:T(128)} %constant.76), dimensions={0}, to_apply=%all_to_all.12.reduce_sub_computation | reduce | bytes 2359300 | tf_op jit(solution)/shard_map/all_to_all | solution.py:106
  94.7 1.1 slice.518
  95.9 1.8 %gather_fusion = f32[16,8,2048]{2,1,0:T(8,128)S(1)} fusion(f32[16,8,2048]{2,1,0:T(8,128)} %slice.518, s32[1024]{0:T(1024)S(1)} %pad_clamp_fusion), kind=kCustom, calls=%fused_computation | custom fusion | bytes 2097216 | tf_op jit(solution)/shard_map/jit(_take)/gather | solution.py:118
  108.1 4.7 %all-to-all-start.1 = ((f32[16,1,8,2048]{3,2,1,0:T(8,128)}), f32[16,1,8,2048]{3,2,1,0:T(8,128)S(1)}, u32[]{:S(2)}, u32[]{:S(2)}) async-start(f32[16,1,8,2048]{3,2,1,0:T(8,128)} %fusion.79), calls=%async_computation.1 | async-start | bytes 2097152 | tf_op jit(solution)/shard_map/all_to_all | solution.py:120
  113.7 23.9 %all-to-all-done.1 = f32[16,1,8,2048]{3,2,1,0:T(8,128)S(1)} async-done(((f32[16,1,8,2048]{3,2,1,0:T(8,128)}), f32[16,1,8,2048]{3,2,1,0:T(8,128)S(1)}, u32[]{:S(2)}, u32[]{:S(2)}) %all-to-all-start.1) | async-done | bytes 1048608 | tf_op jit(solution)/shard_map/all_to_all | solution.py:120
  137.7 1.0 copy.48
  (77 shorter events, 20.6 us)
Async XLA Ops:
  0.6 1.5 %copy-start.3 = (f32[1,128,2048]{2,1,0:T(8,128)S(1)}, f32[1,128,2048]{2,1,0:T(8,128)}, u32[]{:S(2)}) copy-start(f32[1,128,2048]{2,1,0:T(8,128)} %param.7) | copy-start | bytes 3145732
  2.2 2.3 %copy-start.6 = (f32[16]{0:T(128)S(1)}, f32[16]{0:T(128)}, u32[]{:S(2)}) copy-start(f32[16]{0:T(128)} %param.9) | copy-start | bytes 196
  2.3 3.2 %collective-permute-start.1 = (f32[2,3,2048]{2,1,0:T(4,128)S(1)}, f32[2,3,2048]{2,1,0:T(4,128)S(1)}, u32[]{:S(2)}, u32[]{:S(2)}) collective-permute-start(f32[2,3,2048]{2,1,0:T(4,128)S(1)} %get-tuple-element.33), channel_id=1, source_target_pairs={{1,0},{0,1},{3,2},{2,3},{5,4},{4,5},{7,6},{6,7},{9,8},{8,9},{11,10... | collective-permute-start | bytes 147464 | tf_op jit(solution)/shard_map/ppermute | solution.py:21
  3.6 3.9 %collective-permute-start = (f32[2,3,2048]{2,1,0:T(4,128)S(1)}, f32[2,3,2048]{2,1,0:T(4,128)S(1)}, u32[]{:S(2)}, u32[]{:S(2)}) collective-permute-start(f32[2,3,2048]{2,1,0:T(4,128)S(1)} %get-tuple-element.32), channel_id=1, source_target_pairs={{0,1},{1,0},{2,3},{3,2},{4,5},{5,4},{6,7},{7,6},{8,9},{9,8},{10,11... | collective-permute-start | bytes 147464 | tf_op jit(solution)/shard_map/ppermute | solution.py:19
  14.0 3.2 %collective-permute-start.2 = (f32[2,3,2048]{2,1,0:T(4,128)S(1)}, f32[2,3,2048]{2,1,0:T(4,128)S(1)}, u32[]{:S(2)}, u32[]{:S(2)}) collective-permute-start(f32[2,3,2048]{2,1,0:T(4,128)S(1)} %get-tuple-element.30), channel_id=1, source_target_pairs={{0,1},{1,0},{2,3},{3,2},{4,5},{5,4},{6,7},{7,6},{8,9},{9,8},{10,11... | collective-permute-start | bytes 147464 | tf_op jit(solution)/shard_map/ppermute | solution.py:19
  14.6 3.3 %collective-permute-start.3 = (f32[2,3,2048]{2,1,0:T(4,128)S(1)}, f32[2,3,2048]{2,1,0:T(4,128)S(1)}, u32[]{:S(2)}, u32[]{:S(2)}) collective-permute-start(f32[2,3,2048]{2,1,0:T(4,128)S(1)} %get-tuple-element.31), channel_id=1, source_target_pairs={{1,0},{0,1},{3,2},{2,3},{5,4},{4,5},{7,6},{6,7},{9,8},{8,9},{11,10... | collective-permute-start | bytes 147464 | tf_op jit(solution)/shard_map/ppermute | solution.py:21
  24.3 1.0 copy-start.1
  24.4 1.3 copy-start.2
  24.4 2.8 %copy-start.7 = (s32[16]{0:T(128)S(1)}, s32[16]{0:T(128)}, u32[]{:S(2)}) copy-start(s32[16]{0:T(128)} %param.11) | copy-start | bytes 196
  24.4 3.4 %copy-start = (f32[1,128,2048]{2,1,0:T(8,128)S(1)}, f32[1,128,2048]{2,1,0:T(8,128)}, u32[]{:S(2)}) copy-start(f32[1,128,2048]{2,1,0:T(8,128)} %param.6) | copy-start | bytes 3145732
  25.7 4.7 %collective-permute-start.4 = (f32[2,3,2048]{2,1,0:T(4,128)S(1)}, f32[2,3,2048]{2,1,0:T(4,128)S(1)}, u32[]{:S(2)}, u32[]{:S(2)}) collective-permute-start(f32[2,3,2048]{2,1,0:T(4,128)S(1)} %get-tuple-element.28), channel_id=1, source_target_pairs={{0,1},{1,0},{2,3},{3,2},{4,5},{5,4},{6,7},{7,6},{8,9},{9,8},{10,11... | collective-permute-start | bytes 147464 | tf_op jit(solution)/shard_map/ppermute | solution.py:19
  26.4 4.0 %collective-permute-start.5 = (f32[2,3,2048]{2,1,0:T(4,128)S(1)}, f32[2,3,2048]{2,1,0:T(4,128)S(1)}, u32[]{:S(2)}, u32[]{:S(2)}) collective-permute-start(f32[2,3,2048]{2,1,0:T(4,128)S(1)} %get-tuple-element.29), channel_id=1, source_target_pairs={{1,0},{0,1},{3,2},{2,3},{5,4},{4,5},{7,6},{6,7},{9,8},{8,9},{11,10... | collective-permute-start | bytes 147464 | tf_op jit(solution)/shard_map/ppermute | solution.py:21
  36.6 1.2 copy-start.4
  36.7 1.5 %copy-start.5 = (f32[128,2047]{1,0:T(8,128)S(1)}, f32[128,2047]{1,0:T(8,128)}, u32[]{:S(2)}) copy-start(f32[128,2047]{1,0:T(8,128)} %slice.515) | copy-start | bytes 3144196
  108.1 29.6 %all-to-all-start.1 = ((f32[16,1,8,2048]{3,2,1,0:T(8,128)}), f32[16,1,8,2048]{3,2,1,0:T(8,128)S(1)}, u32[]{:S(2)}, u32[]{:S(2)}) async-start(f32[16,1,8,2048]{3,2,1,0:T(8,128)} %fusion.79), calls=%async_computation.1 | async-start | bytes 2097152 | tf_op jit(solution)/shard_map/all_to_all | solution.py:120
